TPU v7x, 32 devices: a whole 2x2x4 slice. The times are simulated.
32 devices in a mesh: grp: 2 (over core), brick: 16 (over z, y, x).
Axes of the slice: x: 2, y: 2, z: 4, core: 2. Of those that a mesh axis runs over, the one named last changes fastest.
Arguments:
- density: float32 [64, 64, 256], P('brick', None, 'grp'), may hold values from 0.5 to 2
- energy_field: float32 [64, 64, 256], P('brick', None, 'grp'), may hold values from -6 to 6
- lepton_field: float32 [64, 64, 256], P('brick', None, 'grp'), may hold values from 0.1 to 0.6
- velocity: float32 [3, 64, 64, 256], P(None, 'brick', None, 'grp'), may hold values from -4 to 4
- abundance: float32 [2, 16, 1024, 128], P('grp', 'brick'), may hold values from -1.2 to 1.2
- tracer_mass: float32 [2, 16, 1024], P('grp', 'brick'), may hold values from 0.2 to 1
- tracer_cell: int32 [2, 16, 1024], P('grp', 'brick'), may hold values from 0 to 32767
- tracer_count: int32 [2, 16], P('grp', 'brick'), may hold values from 1 to 1024, as said below
- weak_rates: float32 [128, 128], replicated, may hold values from -0.5 to 0.5
- capture_rates: float32 [128, 128], replicated, may hold values from -0.5 to 0.5
- binding: float32 [128], replicated, may hold values from -6 to 6
- charge_ratio: float32 [128], replicated, may hold values from 0 to 1
Outputs:
- density_out: float32 [64, 64, 256], P('brick', None, 'grp')
- energy_out: float32 [64, 64, 256], P('brick', None, 'grp')
- lepton_out: float32 [64, 64, 256], P('brick', None, 'grp')
- abundance_out: float32 [2, 16, 1024, 128], P('grp', 'brick')
Inputs may be any that keep to these rules, and one draw needn't show every extreme that they name: `tracer_count`: for each index of grp the counts sum to 8192; exactly one brick of each half holds 1024, the most; every other brick holds at most 512, and some brick of each half holds exactly 512.
All inputs are finite; a program needn't handle non-finite values.
Results may differ from a plain program's by a relative error of at most 0.00029.
Values sent between devices are 32-bit elements; how exact they have to be, the bound alone decides.
A program may use at most 64 MiB of HBM per device.

v0:
```python
import functools

import jax
import jax.numpy as jnp
from jax import lax
from jax.experimental import pallas as pl
from jax.experimental.pallas import tpu as pltpu
from jax.sharding import PartitionSpec as P

NEWTON = 2
SWEEPS = 8
courant = 0.8
f32 = jnp.float32
bf16 = jnp.bfloat16
BLOCK = 256
MESH = pl.DeviceIdType.MESH


def split(values):
    high = values.astype(bf16)
    low = (values - high.astype(f32)).astype(bf16)
    return high, low


def dot(a, b, dims=((1,), (0,))):
    return lax.dot_general(a, b, (dims, ((), ())), preferred_element_type=f32)


def five_point(lower2, lower1, upper1, upper2):
    return 8.0 * (upper1 - lower1) - (upper2 - lower2)


def y_part(g):
    n = g.shape[0]
    return five_point(
        pltpu.roll(g, 2, 0), pltpu.roll(g, 1, 0), pltpu.roll(g, n - 1, 0), pltpu.roll(g, n - 2, 0)
    )


def z_part(h, other):
    n = h.shape[1]
    lane = lax.broadcasted_iota(jnp.int32, h.shape, 1)
    return five_point(
        pltpu.roll(jnp.where(lane >= n - 2, other, h), 2, 1),
        pltpu.roll(jnp.where(lane >= n - 1, other, h), 1, 1),
        pltpu.roll(jnp.where(lane < 1, other, h), n - 1, 1),
        pltpu.roll(jnp.where(lane < 2, other, h), n - 2, 1),
    )


def kernel(
    axis_sizes,
    count_ref,
    rho_ref,
    eps_ref,
    lam_ref,
    vel_ref,
    rows_ref,
    mass_ref,
    cell_ref,
    weak_ref,
    capture_ref,
    table_ref,
    density_out,
    energy_out,
    lepton_out,
    abundance_out,
    xs,
    zs,
    low_in,
    high_in,
    z_in,
    mid,
    weights,
    onehot,
    rate_weak,
    rate_capture,
    start_rows,
    alpha_capture,
    scaled_capture,
    target,
    update,
    deposit,
    send_sem,
    recv_sem,
):
    n_grp, n_brick = axis_sizes
    g = lax.axis_index("grp")
    b = lax.axis_index("brick")
    right = (g, lax.rem(b + 1, n_brick))
    left = (g, lax.rem(b + n_brick - 1, n_brick))
    partner = (lax.rem(g + 1, n_grp), b)
    fields = (rho_ref, eps_ref, lam_ref)
    outs = (density_out, energy_out, lepton_out)
    cx, cy, cz = rho_ref.shape
    capacity, species = rows_ref.shape

    barrier = pltpu.get_barrier_semaphore()
    for neighbour in (left, right, partner):
        pl.semaphore_signal(barrier, inc=1, device_id=neighbour, device_id_type=MESH)

    for f in range(3):
        for p in range(cx):
            xs[0, f, p] = vel_ref[0, p] * fields[f][p]
            zs[0, f, p] = vel_ref[2, p] * fields[f][p]

    pl.semaphore_wait(barrier, 3)

    def copies(stage, f):
        made = []
        for k, (src, dst, device) in enumerate(
            (
                (xs.at[stage, f, pl.ds(0, 2)], high_in.at[stage, f], left),
                (xs.at[stage, f, pl.ds(cx - 2, 2)], low_in.at[stage, f], right),
                (zs.at[stage, f], z_in.at[stage, f], partner),
            )
        ):
            made.append(
                pltpu.make_async_remote_copy(
                    src_ref=src,
                    dst_ref=dst,
                    send_sem=send_sem.at[stage, f, k],
                    recv_sem=recv_sem.at[stage, f, k],
                    device_id=device,
                    device_id_type=MESH,
                )
            )
        return made

    started = [[copies(stage, f) for f in range(3)] for stage in range(2)]
    for f in range(3):
        for copy in started[0][f]:
            copy.start()

    cells = cell_ref[...]
    cell_row = cells // cz
    cell_lane = cells - cell_row * cz
    row_ids = lax.broadcasted_iota(jnp.int32, (cx * cy, capacity), 0)
    onehot[...] = jnp.where(row_ids == cell_row, 1.0, 0.0).astype(bf16)
    lane_ids = lax.broadcasted_iota(jnp.int32, (cz, capacity), 0)
    lane_hit = lane_ids == cell_lane
    picked = []
    for f in range(3):
        high, low = split(fields[f][...].reshape(cx * cy, cz))
        found = dot(high, onehot[...], ((0,), (0,))) + dot(low, onehot[...], ((0,), (0,)))
        picked.append(jnp.sum(jnp.where(lane_hit, found, 0.0), axis=0, keepdims=True))
    rho, eps, lam = picked
    weak_row = 0.62 + 0.04 * rho + 0.05 * (lam / rho)
    capture_row = 0.3 * jax.nn.sigmoid(eps / rho)
    for k in range(capacity // 128):
        part = pl.ds(k * 128, 128)
        cols = slice(k * 128, k * 128 + 128)
        rate_weak[part, :] = jnp.broadcast_to(weak_row[:, cols], (128, 128)).T
        rate_capture[part, :] = jnp.broadcast_to(capture_row[:, cols], (128, 128)).T

    for k, ref in enumerate((weak_ref, capture_ref)):
        high, low = split(ref[...])
        cols = pl.ds(k * species, species)
        weights[0:species, cols] = high
        weights[species : 2 * species, cols] = high
        weights[2 * species : 3 * species, cols] = low

    count = count_ref[0, 0]
    for k in range(capacity // BLOCK):
        part = pl.ds(k * BLOCK, BLOCK)
        row = lax.broadcasted_iota(jnp.int32, (BLOCK, species), 0) + k * BLOCK
        first = jnp.where(row < count, rows_ref[part, :], 0.0)
        start_rows[part, :] = first
        abundance_out[part, :] = first

    def product(values):
        high, low = split(values)
        return dot(jnp.concatenate([high, low, high], axis=1), weights[...])

    def newton(turn):
        for k in range(capacity // BLOCK):
            part = pl.ds(k * BLOCK, BLOCK)
            now = abundance_out[part, :]
            made = product(now)
            capture = made[:, species:]
            scaled = rate_capture[part, :]
            alpha = scaled * now[:, 0:1]
            alpha_capture[part, :] = alpha
            scaled_capture[part, :] = scaled * capture
            aim = rate_weak[part, :] * made[:, :species] + alpha * capture
            if turn:
                aim = aim - (now - start_rows[part, :])
            target[part, :] = aim
            update[part, :] = aim

        def sweep(_, carry):
            for k in range(capacity // BLOCK):
                part = pl.ds(k * BLOCK, BLOCK)
                now = update[part, :]
                made = product(now)
                update[part, :] = target[part, :] + (
                    rate_weak[part, :] * made[:, :species]
                    + alpha_capture[part, :] * made[:, species:]
                    + scaled_capture[part, :] * now[:, 0:1]
                )
            return carry

        lax.fori_loop(0, SWEEPS, sweep, 0)
        for k in range(capacity // BLOCK):
            part = pl.ds(k * BLOCK, BLOCK)
            abundance_out[part, :] = abundance_out[part, :] + update[part, :]

    def tendency(stage, f, field):
        results = []
        line = (
            [low_in[stage, f, 0], low_in[stage, f, 1]]
            + [xs[stage, f, p] for p in range(cx)]
            + [high_in[stage, f, 0], high_in[stage, f, 1]]
        )
        for p in range(cx):
            along_x = five_point(line[p], line[p + 1], line[p + 3], line[p + 4])
            along_y = y_part(vel_ref[1, p] * field[p])
            along_z = z_part(zs[stage, f, p], z_in[stage, f, p])
            results.append((along_x + along_y + along_z) * (-1.0 / 12.0))
        return results

    newton(0)

    for f in range(3):
        for copy in started[0][f]:
            copy.wait_recv()
        slopes = tendency(0, f, [fields[f][p] for p in range(cx)])
        for p in range(cx):
            half = fields[f][p] + 0.5 * courant * slopes[p]
            mid[f, p] = half
            xs[1, f, p] = vel_ref[0, p] * half
            zs[1, f, p] = vel_ref[2, p] * half
        for copy in started[1][f]:
            copy.start()

    newton(1)

    change_high, change_low = split(abundance_out[...] - start_rows[...])
    table_high, table_low = split(table_ref[...])
    gains = (
        dot(table_high, change_high, ((1,), (1,)))
        + dot(table_high, change_low, ((1,), (1,)))
        + dot(table_low, change_high, ((1,), (1,)))
    ) * mass_ref[...]
    for k in range(2):
        placed = jnp.where(lane_hit, gains[k : k + 1, :], 0.0)
        high, low = split(placed)
        deposit[k] = (
            dot(onehot[...], high, ((1,), (1,))) + dot(onehot[...], low, ((1,), (1,)))
        ).reshape(cx, cy, cz)

    for f in range(3):
        for copy in started[1][f]:
            copy.wait_recv()
        slopes = tendency(1, f, [mid[f, p] for p in range(cx)])
        for p in range(cx):
            value = fields[f][p] + courant * slopes[p]
            if f:
                value = value + deposit[f - 1, p]
            outs[f][p] = value

    for stage in range(2):
        for f in range(3):
            for copy in started[stage][f]:
                copy.wait_send()


def on_device(
    axis_sizes,
    density,
    energy_field,
    lepton_field,
    velocity,
    abundance,
    tracer_mass,
    tracer_cell,
    tracer_count,
    weak_rates,
    capture_rates,
    binding,
    charge_ratio,
):
    cx, cy, cz = density.shape
    capacity, species = abundance.shape[2:]
    table = jnp.zeros((8, species), f32).at[0].set(binding).at[1].set(charge_ratio)
    vmem = pl.BlockSpec(memory_space=pltpu.VMEM)
    field = jax.ShapeDtypeStruct(density.shape, f32)
    rows = pltpu.VMEM((capacity, species), f32)
    advanced = pl.pallas_call(
        functools.partial(kernel, axis_sizes),
        out_shape=(field, field, field, jax.ShapeDtypeStruct((capacity, species), f32)),
        in_specs=[pl.BlockSpec(memory_space=pltpu.SMEM)] + [vmem] * 10,
        out_specs=(vmem,) * 4,
        scratch_shapes=[
            pltpu.VMEM((2, 3, cx, cy, cz), f32),
            pltpu.VMEM((2, 3, cx, cy, cz), f32),
            pltpu.VMEM((2, 3, 2, cy, cz), f32),
            pltpu.VMEM((2, 3, 2, cy, cz), f32),
            pltpu.VMEM((2, 3, cx, cy, cz), f32),
            pltpu.VMEM((3, cx, cy, cz), f32),
            pltpu.VMEM((3 * species, 2 * species), bf16),
            pltpu.VMEM((cx * cy, capacity), bf16),
            rows,
            rows,
            rows,
            rows,
            rows,
            rows,
            rows,
            pltpu.VMEM((2, cx, cy, cz), f32),
            pltpu.SemaphoreType.DMA((2, 3, 3)),
            pltpu.SemaphoreType.DMA((2, 3, 3)),
        ],
        compiler_params=pltpu.CompilerParams(collective_id=0, has_side_effects=True),
    )(
        tracer_count,
        density,
        energy_field,
        lepton_field,
        velocity,
        abundance.reshape(capacity, species),
        tracer_mass.reshape(1, capacity),
        tracer_cell.reshape(1, capacity),
        weak_rates,
        capture_rates,
        table,
    )
    return advanced[0], advanced[1], advanced[2], advanced[3][None, None]


def solution(mesh):
    sizes = (mesh.shape["grp"], mesh.shape["brick"])
    assert sizes[0] == 2
    return jax.shard_map(
        functools.partial(on_device, sizes),
        mesh=mesh,
        in_specs=(
            P("brick", None, "grp"),
            P("brick", None, "grp"),
            P("brick", None, "grp"),
            P(None, "brick", None, "grp"),
            P("grp", "brick", None, None),
            P("grp", "brick", None),
            P("grp", "brick", None),
            P("grp", "brick"),
            P(),
            P(),
            P(),
            P(),
        ),
        out_specs=(
            P("brick", None, "grp"),
            P("brick", None, "grp"),
            P("brick", None, "grp"),
            P("grp", "brick", None, None),
        ),
        check_vma=False,
    )
```

profile of v0, /device:TPU:0, one launch (start us, length us, event | category | flops | bytes accessed | tf_op | source)
XLA Modules:
  0.0 36.8 jit_solution(13967013770652743465)
XLA Ops:
  1.3 0.0 copy-start.2
  1.3 0.6 %copy-done.2 = f32[128]{0:T(128)S(1)} copy-done((f32[128]{0:T(128)S(1)}, f32[128]{0:T(128)}, u32[]{:S(2)}) %copy-start.2) | copy-done | bytes 536
  1.9 0.0 copy-start.3
  1.9 0.6 %copy-done.3 = f32[128]{0:T(128)S(1)} copy-done((f32[128]{0:T(128)S(1)}, f32[128]{0:T(128)}, u32[]{:S(2)}) %copy-start.3) | copy-done | bytes 536
  2.6 0.0 copy-start.1
  2.6 0.6 %copy-done.1 = f32[8,128]{1,0:T(8,128)} copy-done((f32[8,128]{1,0:T(8,128)}, f32[8,128]{1,0:T(8,128)S(1)}, u32[]{:S(2)}) %copy-start.1) | copy-done | bytes 4120
  3.2 28.1 %shard_map.147 = (f32[4,64,128]{2,1,0:T(8,128)}, f32[4,64,128]{2,1,0:T(8,128)}, f32[4,64,128]{2,1,0:T(8,128)}, f32[1024,128]{1,0:T(8,128)}) custom-call(s32[1,1]{1,0:T(1,128)S(6)} %copy.21.count_ref, f32[4,64,128]{2,1,0:T(8,128)} %rho_ref.1, f32[4,64,128]{2,1,0:T(8,128)} %eps_ref.1, f32[4,64,128]{2,1,0:T(8,128)} %lam_ref.1, f32[3,4,64,128]{3,2,1,0:T(8,128)} %vel_ref.1, ...), custom_call_target="tpu_custom_call" | custom-call | tf_op jit(solution)/shard_map/pallas_call | solution.py:289
  31.3 0.0 copy-start
  31.3 1.6 %copy.22 = f32[4,64,128]{2,1,0:T(8,128)} copy(f32[4,64,128]{2,1,0:T(8,128)} %get-tuple-element.40) | data formatting | bytes 262144
  32.9 1.6 %copy.23 = f32[4,64,128]{2,1,0:T(8,128)} copy(f32[4,64,128]{2,1,0:T(8,128)} %get-tuple-element.41) | data formatting | bytes 262144
  34.5 1.6 %copy.24 = f32[4,64,128]{2,1,0:T(8,128)} copy(f32[4,64,128]{2,1,0:T(8,128)} %get-tuple-element.42) | data formatting | bytes 262144
  36.0 0.0 copy-done
  36.0 0.8 %copy.25 = f32[1,1,1024,128]{3,2,1,0:T(8,128)} copy(f32[1,1,1024,128]{3,2,1,0:T(8,128)S(1)} %bitcast.7) | data formatting | bytes 1048576
  (2 shorter events, 0.0 us)
Async XLA Ops:
  1.3 0.7 %copy-start.2 = (f32[128]{0:T(128)S(1)}, f32[128]{0:T(128)}, u32[]{:S(2)}) copy-start(f32[128]{0:T(128)} %param.26) | copy-start | bytes 1540
  1.9 0.7 %copy-start.3 = (f32[128]{0:T(128)S(1)}, f32[128]{0:T(128)}, u32[]{:S(2)}) copy-start(f32[128]{0:T(128)} %param.27) | copy-start | bytes 1540
  2.6 0.6 %copy-start.1 = (f32[8,128]{1,0:T(8,128)}, f32[8,128]{1,0:T(8,128)S(1)}, u32[]{:S(2)}) copy-start(f32[8,128]{1,0:T(8,128)S(1)} %scatter.9.table_ref) | copy-start | bytes 12292
  31.3 4.8 %copy-start = (f32[1024,128]{1,0:T(8,128)S(1)}, f32[1024,128]{1,0:T(8,128)}, u32[]{:S(2)}) copy-start(f32[1024,128]{1,0:T(8,128)} %get-tuple-element.35) | copy-start | bytes 1572868
where the time goes:
time: 37.1 us; the launch traced here: 36.8 us
  Pallas kernels  28.1 us (76%)
  local copies, waits for them, and re-layouts  7.48 us (20%)
  between operations  1.31 us (4%)
    pallas_call x1, Pallas kernels, on_device(): pl.pallas_call(functools.partial(kernel, axis_sizes), out_shape=(field, f...  28.1 us
    unnamed x12, local copies, waits for them, and re-layouts  7.45 us

commit v1 on v0

--- a/solution.py
+++ b/solution.py
@@ -60,7 +60,8 @@
     cell_ref,
     weak_ref,
     capture_ref,
-    table_ref,
+    binding_ref,
+    charge_ref,
     density_out,
     energy_out,
     lepton_out,
@@ -236,7 +237,10 @@
     newton(1)
 
     change_high, change_low = split(abundance_out[...] - start_rows[...])
-    table_high, table_low = split(table_ref[...])
+    table = jnp.concatenate(
+        [binding_ref[...], charge_ref[...], jnp.zeros((6, species), f32)], axis=0
+    )
+    table_high, table_low = split(table)
     gains = (
         dot(table_high, change_high, ((1,), (1,)))
         + dot(table_high, change_low, ((1,), (1,)))
@@ -263,6 +267,15 @@
         for f in range(3):
             for copy in started[stage][f]:
                 copy.wait_send()
+
+
+def settle(a_ref, b_ref, c_ref, d_ref, a_out, b_out, c_out, d_out, sem):
+    pairs = ((d_ref, d_out), (a_ref, a_out), (b_ref, b_out), (c_ref, c_out))
+    moves = [pltpu.make_async_copy(src, dst, sem.at[k]) for k, (src, dst) in enumerate(pairs)]
+    for move in moves:
+        move.start()
+    for move in moves:
+        move.wait()
 
 
 def on_device(
@@ -282,14 +295,13 @@
 ):
     cx, cy, cz = density.shape
     capacity, species = abundance.shape[2:]
-    table = jnp.zeros((8, species), f32).at[0].set(binding).at[1].set(charge_ratio)
     vmem = pl.BlockSpec(memory_space=pltpu.VMEM)
     field = jax.ShapeDtypeStruct(density.shape, f32)
     rows = pltpu.VMEM((capacity, species), f32)
     advanced = pl.pallas_call(
         functools.partial(kernel, axis_sizes),
-        out_shape=(field, field, field, jax.ShapeDtypeStruct((capacity, species), f32)),
-        in_specs=[pl.BlockSpec(memory_space=pltpu.SMEM)] + [vmem] * 10,
+        out_shape=(pltpu.VMEM(density.shape, f32),) * 3 + (rows,),
+        in_specs=[pl.BlockSpec(memory_space=pltpu.SMEM)] + [vmem] * 11,
         out_specs=(vmem,) * 4,
         scratch_shapes=[
             pltpu.VMEM((2, 3, cx, cy, cz), f32),
@@ -323,9 +335,18 @@
         tracer_cell.reshape(1, capacity),
         weak_rates,
         capture_rates,
-        table,
-    )
-    return advanced[0], advanced[1], advanced[2], advanced[3][None, None]
+        binding.reshape(1, species),
+        charge_ratio.reshape(1, species),
+    )
+    whole = pl.BlockSpec(memory_space=pl.ANY)
+    results = pl.pallas_call(
+        settle,
+        out_shape=(field, field, field, jax.ShapeDtypeStruct((capacity, species), f32)),
+        in_specs=[whole] * 4,
+        out_specs=(whole,) * 4,
+        scratch_shapes=[pltpu.SemaphoreType.DMA((4,))],
+    )(*[pltpu.with_memory_space_constraint(a, pltpu.VMEM) for a in advanced])
+    return results[0], results[1], results[2], results[3][None, None]
 
 
 def solution(mesh):

time: 37.1 us -> 29.5 us (0.80)
  local copies, waits for them, and re-layouts: 7.48 us -> 0 us
    unnamed x12 -> x0, local copies, waits for them, and re-layouts: 7.45 us -> none
    pallas_call x1 -> x2, Pallas kernels: 28.1 us -> 28.1 us  [the longest x1 27.1 us: on_device(): pl.pallas_call(functools.partial(kernel, axis_sizes), out_shape=(pltpu.VM...]
where the time goes in v1:
time: 29.5 us; the launch traced here: 29.4 us
  Pallas kernels  28.1 us (95%)
  between operations  1.29 us (4%)
    pallas_call x1, Pallas kernels, on_device(): pl.pallas_call(functools.partial(kernel, axis_sizes), out_shape=(pltpu.VM...  27.1 us
    pallas_call x1, Pallas kernels, on_device(): pl.pallas_call(settle, out_shape=(field, field, field, jax.ShapeDtypeStru...  0.95 us

profile of v1, /device:TPU:0, one launch (start us, length us, event | category | flops | bytes accessed | tf_op | source)
XLA Modules:
  0.0 29.4 jit_solution(11694968832075367838)
XLA Ops:
  1.3 27.1 %shard_map.147 = (f32[4,64,128]{2,1,0:T(8,128)S(1)}, f32[4,64,128]{2,1,0:T(8,128)S(1)}, f32[4,64,128]{2,1,0:T(8,128)S(1)}, f32[1024,128]{1,0:T(8,128)S(1)}) custom-call(s32[1,1]{1,0:T(1,128)S(6)} %copy.16.count_ref, f32[4,64,128]{2,1,0:T(8,128)} %rho_ref.1, f32[4,64,128]{2,1,0:T(8,128)} %eps_ref.1, f32[4,64,128]{2,1,0:T(8,128)} %lam_ref.1, ...), custom_call_target="tpu_custom_call" | custom-call | tf_op jit(solution)/shard_map/pallas_call | solution.py:301
  28.4 0.9 %shard_map.148 = (f32[4,64,128]{2,1,0:T(8,128)}, f32[4,64,128]{2,1,0:T(8,128)}, f32[4,64,128]{2,1,0:T(8,128)}, f32[1024,128]{1,0:T(8,128)}) custom-call(f32[4,64,128]{2,1,0:T(8,128)S(1)} %get-tuple-element.12.a_ref, f32[4,64,128]{2,1,0:T(8,128)S(1)} %get-tuple-element.13.b_ref, f32[4,64,128]{2,1,0:T(8,128)S(1)} %get-tuple-element.14.c_ref, ...), custom_call_target="tpu_custom_call" | custom-call | tf_op jit(solution)/shard_map/pallas_call | solution.py:342

commit v2 on v1

--- a/solution.py
+++ b/solution.py
@@ -173,7 +173,7 @@
         high, low = split(values)
         return dot(jnp.concatenate([high, low, high], axis=1), weights[...])
 
-    def newton(turn):
+    def newton_start(turn):
         for k in range(capacity // BLOCK):
             part = pl.ds(k * BLOCK, BLOCK)
             now = abundance_out[part, :]
@@ -189,6 +189,7 @@
             target[part, :] = aim
             update[part, :] = aim
 
+    def sweeps(number):
         def sweep(_, carry):
             for k in range(capacity // BLOCK):
                 part = pl.ds(k * BLOCK, BLOCK)
@@ -201,7 +202,9 @@
                 )
             return carry
 
-        lax.fori_loop(0, SWEEPS, sweep, 0)
+        lax.fori_loop(0, number, sweep, 0)
+
+    def newton_end():
         for k in range(capacity // BLOCK):
             part = pl.ds(k * BLOCK, BLOCK)
             abundance_out[part, :] = abundance_out[part, :] + update[part, :]
@@ -220,9 +223,7 @@
             results.append((along_x + along_y + along_z) * (-1.0 / 12.0))
         return results
 
-    newton(0)
-
-    for f in range(3):
+    def half_step(f):
         for copy in started[0][f]:
             copy.wait_recv()
         slopes = tendency(0, f, [fields[f][p] for p in range(cx)])
@@ -234,7 +235,16 @@
         for copy in started[1][f]:
             copy.start()
 
-    newton(1)
+    newton_start(0)
+    sweeps(SWEEPS)
+    newton_end()
+    half_step(0)
+    newton_start(1)
+    sweeps(SWEEPS // 2)
+    half_step(1)
+    sweeps(SWEEPS - SWEEPS // 2)
+    newton_end()
+    half_step(2)
 
     change_high, change_low = split(abundance_out[...] - start_rows[...])
     table = jnp.concatenate(

time: 29.5 us -> 27.5 us (0.932)
  Pallas kernels: 28.1 us -> 26.1 us
    pallas_call x1, Pallas kernels: 27.1 us -> 25.1 us  [on_device(): pl.pallas_call(functools.partial(kernel, axis_sizes), out_shape=(pltpu.VM...]
where the time goes in v2:
time: 27.5 us; the launch traced here: 27.3 us
  Pallas kernels  26.1 us (95%)
  between operations  1.29 us (5%)
    pallas_call x1, Pallas kernels, on_device(): pl.pallas_call(functools.partial(kernel, axis_sizes), out_shape=(pltpu.VM...  25.1 us
    pallas_call x1, Pallas kernels, on_device(): pl.pallas_call(settle, out_shape=(field, field, field, jax.ShapeDtypeStru...  0.95 us

profile of v2, /device:TPU:0, one launch (start us, length us, event | category | flops | bytes accessed | tf_op | source)
XLA Modules:
  0.0 27.3 jit_solution(12680132954511036690)
XLA Ops:
  1.3 25.1 %shard_map.147 = (f32[4,64,128]{2,1,0:T(8,128)S(1)}, f32[4,64,128]{2,1,0:T(8,128)S(1)}, f32[4,64,128]{2,1,0:T(8,128)S(1)}, f32[1024,128]{1,0:T(8,128)S(1)}) custom-call(s32[1,1]{1,0:T(1,128)S(6)} %copy.16.count_ref, f32[4,64,128]{2,1,0:T(8,128)} %rho_ref.1, f32[4,64,128]{2,1,0:T(8,128)} %eps_ref.1, f32[4,64,128]{2,1,0:T(8,128)} %lam_ref.1, ...), custom_call_target="tpu_custom_call" | custom-call | tf_op jit(solution)/shard_map/pallas_call | solution.py:311
  26.4 0.9 %shard_map.148 = (f32[4,64,128]{2,1,0:T(8,128)}, f32[4,64,128]{2,1,0:T(8,128)}, f32[4,64,128]{2,1,0:T(8,128)}, f32[1024,128]{1,0:T(8,128)}) custom-call(f32[4,64,128]{2,1,0:T(8,128)S(1)} %get-tuple-element.12.a_ref, f32[4,64,128]{2,1,0:T(8,128)S(1)} %get-tuple-element.13.b_ref, f32[4,64,128]{2,1,0:T(8,128)S(1)} %get-tuple-element.14.c_ref, ...), custom_call_target="tpu_custom_call" | custom-call | tf_op jit(solution)/shard_map/pallas_call | solution.py:352
